TPU v7x, 512 devices: a whole 4x8x8 slice. The times are simulated.
512 devices in a mesh: seq: 16 (over y, core), doc: 32 (over z, x).
Axes of the slice: x: 4, y: 8, z: 8, core: 2. Of those that a mesh axis runs over, the one named last changes fastest.
Arguments:
- queries: bfloat16 [262144, 512], P(('doc', 'seq')), parts along dimension 0, may hold values from -64 to 64
- keys: bfloat16 [262144, 512], P(('doc', 'seq')), parts along dimension 0, may hold values from -6 to 6
- values: bfloat16 [262144, 512], P(('doc', 'seq')), parts along dimension 0, may hold values from -6 to 6
- rates: float32 [262144], P(('doc', 'seq')), parts along dimension 0, may hold values from 0.1 to 1
- lengths: int32 [128], P('doc'), parts along dimension 0, may hold values from 1 to 4096, 8192 in all
- norm_gain: float32 [16384], P('doc'), parts along dimension 0, may hold values from 0.5 to 1.5
- w_gate: bfloat16 [16384, 512], P('doc'), parts along dimension 0, may hold values from -0.25 to 0.25
- w_up: bfloat16 [16384, 512], P('doc'), parts along dimension 0, may hold values from -0.25 to 0.25
- w_down: bfloat16 [16384, 512], P('doc'), parts along dimension 0, may hold values from -0.25 to 0.25
- mom_gate: float32 [16384, 512], P('doc', 'seq'), parts along dimension 0, may hold values from -3 to 3
- mom_up: float32 [16384, 512], P('doc', 'seq'), parts along dimension 0, may hold values from -3 to 3
- mom_down: float32 [16384, 512], P('doc', 'seq'), parts along dimension 0, may hold values from -3 to 3
Outputs:
- mixed: bfloat16 [262144, 512], P(('doc', 'seq')), parts along dimension 0
- new_mom_gate: float32 [16384, 512], P('doc', 'seq'), parts along dimension 0
- new_mom_up: float32 [16384, 512], P('doc', 'seq'), parts along dimension 0
- new_mom_down: float32 [16384, 512], P('doc', 'seq'), parts along dimension 0
There are 32 independent parts, one for each index of `doc`. A program takes and returns all parts, laid end to end along the dimension named above; each array names one. Nothing has to cross between parts.
All inputs are finite; a program needn't handle non-finite values.
Results may differ from a plain program's by a relative error of at most 0.019.
Values may be sent and summed in bfloat16 or wider, within the bound.
No kernel may reach another device: no remote copies, remote signals or barrier semaphores. Data moves between devices by JAX's collectives and lax.ppermute only.
A program may use at most 64 MiB of HBM per device.

v0:
```python
import jax
import jax.numpy as jnp
from jax import lax
from jax.sharding import PartitionSpec as P

WIN = 1024
momentum_decay = 0.9
step_size = 0.5


def shifted(block, axis, distance):
    devices = range(lax.axis_size(axis))
    route = [(i - distance, i) for i in devices if i - distance in devices]
    return lax.ppermute(block, axis, route)


def doc_ids(positions, ends):
    return jnp.sum((positions[:, None] >= ends[None, :]).astype(jnp.int32), axis=1)


def window_attention(qblk, kblk, vblk, qpos, kpos, ends):
    scores = jnp.dot(qblk, kblk.T, preferred_element_type=jnp.float32) * qblk.shape[1] ** (-0.5)
    same = doc_ids(qpos, ends)[:, None] == doc_ids(kpos, ends)[None, :]
    delta = qpos[:, None] - kpos[None, :]
    live = same & (delta >= 0) & (delta < WIN) & (kpos[None, :] >= 0)
    scores = jnp.where(live, scores, jnp.float32(-1e30))
    top = jnp.max(scores, axis=1, keepdims=True)
    weights = jnp.where(live, jnp.exp(scores - top), jnp.float32(0.0))
    total = jnp.sum(weights, axis=1, keepdims=True)
    probs = (weights / total).astype(jnp.bfloat16)
    return jnp.dot(probs, vblk, preferred_element_type=jnp.float32)


def silu_parts(gate):
    sig = jax.nn.sigmoid(gate)
    return (gate * sig, sig * (1.0 + gate * (1.0 - sig)))


def step_weight(weight, moment):
    normed = moment * lax.rsqrt(jnp.sum(moment * moment, axis=0, keepdims=True) + 1e-06)
    return (weight.astype(jnp.float32) - step_size * normed).astype(jnp.bfloat16)


def local(
    queries,
    keys,
    values,
    rates,
    lengths,
    norm_gain,
    w_gate,
    w_up,
    w_down,
    mom_gate,
    mom_up,
    mom_down,
):
    tok, width = queries.shape
    index = lax.axis_index("seq")
    ends = jnp.cumsum(lengths)
    reach = (WIN + tok - 1) // tok
    paired = jnp.stack((keys, values))
    earlier = [shifted(paired, "seq", hops) for hops in range(reach, 0, -1)]
    buffer = jnp.concatenate(earlier + [paired], axis=1)
    halo_len = reach * tok
    first = index * tok
    begin = halo_len - WIN
    qpos = first + 0 + jnp.arange(tok, dtype=jnp.int32)
    kpos = first + 0 - WIN + jnp.arange(tok + WIN, dtype=jnp.int32)
    pieces = window_attention(
        queries,
        buffer[0, begin : begin + tok + WIN],
        buffer[1, begin : begin + tok + WIN],
        qpos,
        kpos,
        ends,
    )
    gate = jnp.dot(keys, w_gate, preferred_element_type=jnp.float32)
    upper = jnp.dot(keys, w_up, preferred_element_type=jnp.float32)
    act, slope = silu_parts(gate)
    hidden = (act * upper).astype(jnp.bfloat16)
    err = (-(rates[:, None] * values.astype(jnp.float32))).astype(jnp.bfloat16)
    back = jnp.dot(err, w_down.T, preferred_element_type=jnp.float32)
    d_up = (back * act).astype(jnp.bfloat16)
    d_gate = (back * upper * slope).astype(jnp.bfloat16)
    part_gate = jnp.dot(keys.T, d_gate, preferred_element_type=jnp.float32)
    part_up = jnp.dot(keys.T, d_up, preferred_element_type=jnp.float32)
    part_down = jnp.dot(hidden.T, err, preferred_element_type=jnp.float32)
    scale = float(tok * lax.axis_size("seq")) ** (-0.5)
    hid_cols = mom_gate.shape[1]
    out_cols = mom_down.shape[1]
    sum_gate, sum_up, sum_down = (
        lax.psum_scatter(
            part_gate.astype(jnp.bfloat16), "seq", scatter_dimension=1, tiled=True
        ).astype(jnp.float32),
        lax.psum_scatter(
            part_up.astype(jnp.bfloat16), "seq", scatter_dimension=1, tiled=True
        ).astype(jnp.float32),
        lax.psum_scatter(
            part_down.astype(jnp.bfloat16), "seq", scatter_dimension=1, tiled=True
        ).astype(jnp.float32),
    )
    new_mom_gate = momentum_decay * mom_gate + sum_gate * scale
    new_mom_up = momentum_decay * mom_up + sum_up * scale
    new_mom_down = momentum_decay * mom_down + sum_down * scale
    shard_gate = step_weight(
        lax.dynamic_slice_in_dim(w_gate, index * hid_cols, hid_cols, 1), new_mom_gate
    )
    shard_up = step_weight(
        lax.dynamic_slice_in_dim(w_up, index * hid_cols, hid_cols, 1), new_mom_up
    )
    shard_down = step_weight(
        lax.dynamic_slice_in_dim(w_down, index * out_cols, out_cols, 1), new_mom_down
    )
    gate_new, up_new, down_new = (
        lax.all_gather(shard_gate, "seq", axis=1, tiled=True),
        lax.all_gather(shard_up, "seq", axis=1, tiled=True),
        lax.all_gather(shard_down, "seq", axis=1, tiled=True),
    )
    qa = jnp.dot(queries, gate_new, preferred_element_type=jnp.float32)
    qb = jnp.dot(queries, up_new, preferred_element_type=jnp.float32)
    qh = (jax.nn.silu(qa) * qb).astype(jnp.bfloat16)
    fast = jnp.dot(qh, down_new, preferred_element_type=jnp.float32)
    normed = fast * lax.rsqrt(jnp.mean(fast * fast, axis=1, keepdims=True) + 1e-06) * norm_gain
    mixed = (pieces + normed).astype(jnp.bfloat16)
    return (mixed, new_mom_gate, new_mom_up, new_mom_down)


def solution(mesh):
    in_specs = (
        P(("doc", "seq"), None),
        P(("doc", "seq"), None),
        P(("doc", "seq"), None),
        P(("doc", "seq")),
        P("doc"),
        P("doc"),
        P("doc", None),
        P("doc", None),
        P("doc", None),
        P("doc", "seq"),
        P("doc", "seq"),
        P("doc", "seq"),
    )
    out_specs = (P(("doc", "seq"), None), P("doc", "seq"), P("doc", "seq"), P("doc", "seq"))
    return jax.shard_map(local, mesh=mesh, in_specs=in_specs, out_specs=out_specs, check_vma=False)
```

profile of v0, /device:TPU:1, one launch (start us, length us, event | category | flops | bytes accessed | tf_op | source)
XLA Modules:
  0.0 261.2 jit_solution(15479746361720381000)
XLA Ops:
  7.2 1.7 fusion.32
  9.0 2.1 fusion.23
  11.1 1.3 fusion.13
  13.9 2.9 %fusion.12 = bf16[512,512]{0,1:T(8,128)(2,1)} fusion(bf16[512,512]{1,0:T(8,128)(2,1)S(1)} %copy-done.1, f32[512,512]{1,0:T(8,128)} %copy-done.3, f32[512,512]{1,0:T(8,128)S(1)} %fusion.23, f32[512,512]{1,0:T(8,128)S(1)} %fusion.31), kind=kOutput, calls=%fused_computation.25 | convolution fusion | flops 271319040 | bytes 4194304 | tf_op jit(solution)/shard_map/dot_general | solution.py:86
  17.0 4.6 %collective-permute-start.1 = (bf16[2,512,512]{2,1,0:T(8,128)(2,1)S(1)}, bf16[2,512,512]{2,1,0:T(8,128)(2,1)}, u32[]{:S(2)}, u32[]{:S(2)}) collective-permute-start(bf16[2,512,512]{2,1,0:T(8,128)(2,1)S(1)} %pad_maximum_fusion), channel_id=1, source_target_pairs={{0,32},{32,64},{64,96},{96,128},{128,160},{160,192},{192,224},{224... | collective-permute-start | bytes 3145736 | tf_op jit(solution)/shard_map/ppermute | solution.py:14
  21.6 4.2 %collective-permute-start = (bf16[2,512,512]{2,1,0:T(8,128)(2,1)S(1)}, bf16[2,512,512]{2,1,0:T(8,128)(2,1)}, u32[]{:S(2)}, u32[]{:S(2)}) collective-permute-start(bf16[2,512,512]{2,1,0:T(8,128)(2,1)S(1)} %pad_maximum_fusion), channel_id=1, source_target_pairs={{0,64},{32,96},{64,128},{96,160},{128,192},{160,224},{192,256},{22... | collective-permute-start | bytes 3145736 | tf_op jit(solution)/shard_map/ppermute | solution.py:14
  25.8 3.1 %convolution_convert_fusion = bf16[512,512]{0,1:T(8,128)(2,1)} fusion(f32[512,512]{1,0:T(8,128)} %copy-done.5, f32[512,512]{1,0:T(8,128)} %copy-done.3, bf16[512,512]{1,0:T(8,128)(2,1)S(1)} %copy-done.2, f32[512]{0:T(512)S(1)} %copy-done.14), kind=kOutput, calls=%fused_computation.20 | convolution fusion | flops 271319040 | bytes 3147776 | tf_op jit(solution)/shard_map/dot_general | solution.py:88
  29.5 1.0 constant_dynamic-slice_fusion.2
  30.5 1.0 constant_dynamic-slice_fusion
  33.4 42.8 %reduce-scatter.6.cloned.1.call-done = bf16[512,32]{0,1:T(8,128)(2,1)} async-done(((bf16[512,512]{0,1:T(8,128)(2,1)}), bf16[512,32]{0,1:T(8,128)(2,1)}) %reduce-scatter.6.cloned.1.call-update) | async-done | bytes 32784 | tf_op jit(solution)/shard_map/reduce_scatter | solution.py:96
  76.2 1.0 multiply_reduce_fusion.2
  77.2 60.9 %reduce-scatter.4.cloned.1.call-done = bf16[512,32]{0,1:T(8,128)(2,1)} async-done(((bf16[512,512]{0,1:T(8,128)(2,1)}), bf16[512,32]{0,1:T(8,128)(2,1)}) %reduce-scatter.4.cloned.1.call-update) | async-done | bytes 32784 | tf_op jit(solution)/shard_map/reduce_scatter | solution.py:93
  138.1 1.0 multiply_reduce_fusion.3
  139.2 17.9 %all_gather.10 = bf16[512,512]{0,1:T(8,128)(2,1)S(1)} all-gather(bf16[512,32]{0,1:T(8,128)(2,1)S(1)} %subtract_convert_fusion.1), channel_id=1, replica_groups=mesh['seq'=16,'doc'=32] {'seq'}, dimensions={1}, use_global_device_ids=true | all-gather | bytes 557056 | tf_op jit(solution)/shard_map/all_gather | solution.py:117
  157.1 43.1 %reduce-scatter.8.cloned.1.call-done = bf16[512,32]{0,1:T(8,128)(2,1)} async-done(((bf16[512,512]{0,1:T(8,128)(2,1)}), bf16[512,32]{0,1:T(8,128)(2,1)}) %reduce-scatter.8.cloned.1.call-update) | async-done | bytes 32784 | tf_op jit(solution)/shard_map/reduce_scatter | solution.py:99
  201.2 19.3 %all_gather.11 = bf16[512,512]{0,1:T(8,128)(2,1)} all-gather(bf16[512,32]{0,1:T(8,128)(2,1)S(1)} %subtract_convert_fusion), channel_id=1, replica_groups=mesh['seq'=16,'doc'=32] {'seq'}, dimensions={1}, use_global_device_ids=true | all-gather | bytes 557056 | tf_op jit(solution)/shard_map/all_gather | solution.py:118
  221.3 17.4 %all_gather.9 = bf16[512,512]{0,1:T(8,128)(2,1)S(1)} all-gather(bf16[512,32]{0,1:T(8,128)(2,1)S(1)} %subtract_convert_fusion.2), channel_id=1, replica_groups=mesh['seq'=16,'doc'=32] {'seq'}, dimensions={1}, use_global_device_ids=true | all-gather | bytes 557056 | tf_op jit(solution)/shard_map/all_gather | solution.py:116
  238.7 1.5 convolution_bitcast_fusion.1
  240.2 3.3 %multiply_reduce_fusion = (f32[512]{0:T(512)S(1)}, f32[512,512]{0,1:T(8,128)}) fusion(bf16[512,512]{0,1:T(8,128)(2,1)} %all_gather.11, bf16[512,512]{0,1:T(8,128)(2,1)S(1)} %all_gather.10, bf16[512,512]{1,0:T(8,128)(2,1)S(1)} %copy-done, f32[512,512]{1,0:T(8,128)} %convolution_bitcast_fusion.1), kind=kOutput, calls=%fused_computation.28 | convolution fusion | flops 538967552 | bytes 3672064 | tf_op jit(solution)/shard_map/dot_general | solution.py:123
  243.4 2.5 copy.25
  246.0 1.7 maximum_maximum_fusion
  247.8 1.8 fusion.30
  249.6 1.9 fusion.5
  251.6 3.1 %fusion.9 = bf16[512,512]{1,0:T(8,128)(2,1)} fusion(bf16[2,1536,512]{2,1,0:T(8,128)(2,1)S(1)} %maximum_maximum_fusion, f32[512,1536]{0,1:T(8,128)S(1)} %get-tuple-element.11, f32[512]{0:T(512)S(1)} %fusion.5, f32[512]{0:T(512)S(1)} %get-tuple-element.10, f32[512,512]{1,0:T(8,128)S(1)} %copy-done.4, f32[512]{0:T(512)S(1)} %copy-done.15, ...), kind=kOutput, calls=%fused_computation.19 | convolution fusion | flops 815005696 | bytes 6322176 | tf_op jit(solution)/shard_map/dot_general | solution.py:31
  (61 shorter events, 6.1 us)
Async XLA Ops:
  7.2 231.5 %copy-start = (bf16[512,512]{1,0:T(8,128)(2,1)S(1)}, bf16[512,512]{1,0:T(8,128)(2,1)}, u32[]{:S(2)}) copy-start(bf16[512,512]{1,0:T(8,128)(2,1)} %param.12) | copy-start | bytes 1572868
  7.2 3.9 %copy-start.1 = (bf16[512,512]{1,0:T(8,128)(2,1)S(1)}, bf16[512,512]{1,0:T(8,128)(2,1)}, u32[]{:S(2)}) copy-start(bf16[512,512]{1,0:T(8,128)(2,1)} %param.13) | copy-start | bytes 1572868
  7.2 69.0 %reduce-scatter.6.cloned.1.call-start = ((), (), s32[]{:S(2)}) async-start(), calls=%async_computation.4 | async-start | bytes 557056 | tf_op jit(solution)/shard_map/reduce_scatter | solution.py:96
  9.0 2.1 copy-start.3
  11.1 1.4 copy-start.6
  12.4 125.7 %reduce-scatter.4.cloned.1.call-start = ((), (), s32[]{:S(2)}) async-start(), calls=%async_computation.3 | async-start | bytes 557056 | tf_op jit(solution)/shard_map/reduce_scatter | solution.py:93
  12.9 1.0 copy-start.5
  13.9 2.9 %copy-start.2 = (bf16[512,512]{1,0:T(8,128)(2,1)S(1)}, bf16[512,512]{1,0:T(8,128)(2,1)}, u32[]{:S(2)}) copy-start(bf16[512,512]{1,0:T(8,128)(2,1)} %param.14) | copy-start | bytes 1572868
  13.9 11.9 %copy-start.14 = (f32[512]{0:T(512)S(1)}, f32[512]{0:T(512)}, u32[]{:S(2)}) copy-start(f32[512]{0:T(512)} %param.15) | copy-start | bytes 6148
  16.8 183.3 %reduce-scatter.8.cloned.1.call-start = ((), (), s32[]{:S(2)}) async-start(), calls=%async_computation.5 | async-start | bytes 557056 | tf_op jit(solution)/shard_map/reduce_scatter | solution.py:99
  17.0 14.6 %copy-start.16 = (s32[4]{0:T(128)S(1)}, s32[4]{0:T(128)}, u32[]{:S(2)}) copy-start(s32[4]{0:T(128)} %param.16) | copy-start | bytes 52
  17.0 229.0 %collective-permute-start.1 = (bf16[2,512,512]{2,1,0:T(8,128)(2,1)S(1)}, bf16[2,512,512]{2,1,0:T(8,128)(2,1)}, u32[]{:S(2)}, u32[]{:S(2)}) collective-permute-start(bf16[2,512,512]{2,1,0:T(8,128)(2,1)S(1)} %pad_maximum_fusion), channel_id=1, source_target_pairs={{0,32},{32,64},{64,96},{96,128},{128,160},{160,192},{192,224},{224... | collective-permute-start | bytes 3145736 | tf_op jit(solution)/shard_map/ppermute | solution.py:14
  21.6 224.5 %collective-permute-start = (bf16[2,512,512]{2,1,0:T(8,128)(2,1)S(1)}, bf16[2,512,512]{2,1,0:T(8,128)(2,1)}, u32[]{:S(2)}, u32[]{:S(2)}) collective-permute-start(bf16[2,512,512]{2,1,0:T(8,128)(2,1)S(1)} %pad_maximum_fusion), channel_id=1, source_target_pairs={{0,64},{32,96},{64,128},{96,160},{128,192},{160,224},{192,256},{22... | collective-permute-start | bytes 3145736 | tf_op jit(solution)/shard_map/ppermute | solution.py:14
  28.9 2.8 %copy-start.10 = (s32[512]{0:T(512)}, s32[512]{0:T(512)S(1)}, u32[]{:S(2)}) copy-start(s32[512]{0:T(512)S(1)} %iota_add_fusion.1) | copy-start | bytes 6148
  77.2 166.2 %copy-start.7 = (f32[512,32]{0,1:T(8,128)}, f32[512,32]{0,1:T(8,128)S(1)}, u32[]{:S(2)}) copy-start(f32[512,32]{0,1:T(8,128)S(1)} %get-tuple-element.7) | copy-start | bytes 196612
  139.1 104.3 %copy-start.8 = (f32[512,32]{0,1:T(8,128)}, f32[512,32]{0,1:T(8,128)S(1)}, u32[]{:S(2)}) copy-start(f32[512,32]{0,1:T(8,128)S(1)} %get-tuple-element.5) | copy-start | bytes 196612
  201.1 42.3 %copy-start.9 = (f32[512,32]{0,1:T(8,128)}, f32[512,32]{0,1:T(8,128)S(1)}, u32[]{:S(2)}) copy-start(f32[512,32]{0,1:T(8,128)S(1)} %get-tuple-element.9) | copy-start | bytes 196612
  246.0 1.8 copy-start.11
  246.0 1.8 copy-start.12
  246.0 1.8 copy-start.13
  249.6 1.9 copy-start.4
  249.6 1.9 copy-start.15
Sparse Core Ops, SparseCore 0:
  12.6 63.6 reduce-scatter.5
  79.0 59.0 reduce-scatter.3
  141.5 58.6 reduce-scatter.7
where the time goes:
time: 262 us; the launch traced here: 261 us
  waiting for transfers between devices  147 us (56%)
  blocking collectives  54.5 us (21%)
  matrix products  21.2 us (8%)
  between operations  14.1 us (5%)
  other arithmetic  9.19 us (4%)
  starting transfers between devices  8.92 us (3%)
  local copies, waits for them, and re-layouts  6.51 us (2%)
    reduce_scatter x1, waiting for transfers between devices, local(): lax.psum_scatter(part_gate.astype(jnp.bfloat16), 'seq', scatter_dimension...  60.9 us
    reduce_scatter x1, waiting for transfers between devices, local(): lax.psum_scatter(part_down.astype(jnp.bfloat16), 'seq', scatter_dimension...  43.1 us
    reduce_scatter x1, waiting for transfers between devices, local(): lax.psum_scatter(part_up.astype(jnp.bfloat16), 'seq', scatter_dimension=1...  42.8 us
    all_gather x1, blocking collectives, local(): lax.all_gather(shard_down, 'seq', axis=1, tiled=True)  19.3 us
    all_gather x1, blocking collectives, local(): lax.all_gather(shard_up, 'seq', axis=1, tiled=True)  17.9 us
    all_gather x1, blocking collectives, local(): lax.all_gather(shard_gate, 'seq', axis=1, tiled=True)  17.4 us
    ppermute x2, starting transfers between devices, shifted(): return lax.ppermute(block, axis, route)  8.8 us
  transfers between devices with their start and end apart: 5, of which 3 were waited for; matrix products, arithmetic and copies ran while one was open for 8% of the time, Pallas kernels for 0%

commit v1 on v0

--- a/solution.py
+++ b/solution.py
@@ -6,6 +6,24 @@
 WIN = 1024
 momentum_decay = 0.9
 step_size = 0.5
+
+
+def gather_around(array, axis, dim):
+    ways, here, step = (lax.axis_size(axis), lax.axis_index(axis), array.shape[dim])
+    shape = [n * ways if d == dim else n for d, n in enumerate(array.shape)]
+    full = lax.dynamic_update_slice_in_dim(
+        jnp.zeros(shape, array.dtype), array, here * step, axis=dim
+    )
+    going_up = going_down = array
+    for far in range(1, ways // 2 + 1):
+        going_up = lax.ppermute(going_up, axis, [(d, (d + 1) % ways) for d in range(ways)])
+        full = lax.dynamic_update_slice_in_dim(full, going_up, (here - far) % ways * step, axis=dim)
+        if 2 * far < ways:
+            going_down = lax.ppermute(going_down, axis, [(d, (d - 1) % ways) for d in range(ways)])
+            full = lax.dynamic_update_slice_in_dim(
+                full, going_down, (here + far) % ways * step, axis=dim
+            )
+    return full
 
 
 def shifted(block, axis, distance):
@@ -115,7 +133,7 @@
     gate_new, up_new, down_new = (
         lax.all_gather(shard_gate, "seq", axis=1, tiled=True),
         lax.all_gather(shard_up, "seq", axis=1, tiled=True),
-        lax.all_gather(shard_down, "seq", axis=1, tiled=True),
+        gather_around(shard_down, "seq", 1),
     )
     qa = jnp.dot(queries, gate_new, preferred_element_type=jnp.float32)
     qb = jnp.dot(queries, up_new, preferred_element_type=jnp.float32)

time: 262 us -> 282 us (1.076)
  starting transfers between devices: 8.92 us -> 30.3 us
  blocking collectives: 54.5 us -> 36.6 us
  waiting for transfers between devices: 147 us -> 162 us
    ppermute x0 -> x15, starting transfers between devices: none -> 21.3 us  [the longest x7 17.3 us: gather_around(): lax.ppermute(going_down, axis, [(d, (d - 1) % ways) for d in range(ways)])]
    all_gather x1 -> x0, blocking collectives: 19.3 us -> none  [local(): lax.all_gather(shard_down, 'seq', axis=1, tiled=True)]
    ppermute x0 -> x15, waiting for transfers between devices: none -> 9.04 us  [the longest x8 8.46 us: gather_around(): lax.ppermute(going_up, axis, [(d, (d + 1) % ways) for d in range(ways)])]
    reduce_scatter x1, waiting for transfers between devices: 42.8 us -> 51.6 us  [local(): lax.psum_scatter(part_up.astype(jnp.bfloat16), 'seq', scatter_dimension=1...]
    reduce_scatter x1, waiting for transfers between devices: 60.9 us -> 55.8 us  [local(): lax.psum_scatter(part_gate.astype(jnp.bfloat16), 'seq', scatter_dimension...]
  transfers between devices with their start and end apart: 5 -> 20, of which waited for: 3 -> 14; matrix products, arithmetic and copies ran while one was open for 8% -> 8% of each run, Pallas kernels for 0% -> 0%
where the time goes in v1:
time: 282 us; the launch traced here: 279 us
  waiting for transfers between devices  162 us (57%)
  blocking collectives  36.6 us (13%)
  starting transfers between devices  30.3 us (11%)
  matrix products  21.3 us (8%)
  between operations  14.5 us (5%)
  other arithmetic  8.9 us (3%)
  local copies, waits for them, and re-layouts  5.81 us (2%)
    reduce_scatter x1, waiting for transfers between devices, local(): lax.psum_scatter(part_gate.astype(jnp.bfloat16), 'seq', scatter_dimension...  55.8 us
    reduce_scatter x1, waiting for transfers between devices, local(): lax.psum_scatter(part_up.astype(jnp.bfloat16), 'seq', scatter_dimension=1...  51.6 us
    reduce_scatter x1, waiting for transfers between devices, local(): lax.psum_scatter(part_down.astype(jnp.bfloat16), 'seq', scatter_dimension...  45.3 us
    all_gather x1, blocking collectives, local(): lax.all_gather(shard_up, 'seq', axis=1, tiled=True)  18.7 us
    all_gather x1, blocking collectives, local(): lax.all_gather(shard_gate, 'seq', axis=1, tiled=True)  17.9 us
    ppermute x7, starting transfers between devices, gather_around(): lax.ppermute(going_down, axis, [(d, (d - 1) % ways) for d in range(ways)])  17.3 us
    ppermute x2, starting transfers between devices, shifted(): return lax.ppermute(block, axis, route)  8.89 us
    ppermute x8, waiting for transfers between devices, gather_around(): lax.ppermute(going_up, axis, [(d, (d + 1) % ways) for d in range(ways)])  8.46 us
  transfers between devices with their start and end apart: 20, of which 14 were waited for; matrix products, arithmetic and copies ran while one was open for 8% of the time, Pallas kernels for 0%

profile of v1, /device:TPU:1, one launch (start us, length us, event | category | flops | bytes accessed | tf_op | source)
XLA Modules:
  0.0 279.1 jit_solution(14308296063035355260)
XLA Ops:
  7.2 1.7 fusion.29
  9.0 2.0 fusion.30
  14.1 2.5 fusion.11
  17.8 4.7 %collective-permute-start.1 = (bf16[2,512,512]{2,1,0:T(8,128)(2,1)}, bf16[2,512,512]{2,1,0:T(8,128)(2,1)}, u32[]{:S(2)}, u32[]{:S(2)}) collective-permute-start(bf16[2,512,512]{2,1,0:T(8,128)(2,1)} %pad_maximum_fusion), channel_id=1, source_target_pairs={{0,32},{32,64},{64,96},{96,128},{128,160},{160,192},{192,224},{224... | collective-permute-start | bytes 3145736 | tf_op jit(solution)/shard_map/ppermute | solution.py:32
  22.5 4.2 %collective-permute-start = (bf16[2,512,512]{2,1,0:T(8,128)(2,1)}, bf16[2,512,512]{2,1,0:T(8,128)(2,1)}, u32[]{:S(2)}, u32[]{:S(2)}) collective-permute-start(bf16[2,512,512]{2,1,0:T(8,128)(2,1)} %pad_maximum_fusion), channel_id=1, source_target_pairs={{0,64},{32,96},{64,128},{96,160},{128,192},{160,224},{192,256},{22... | collective-permute-start | bytes 3145736 | tf_op jit(solution)/shard_map/ppermute | solution.py:32
  26.7 3.1 %fusion.10 = bf16[512,512]{0,1:T(8,128)(2,1)} fusion(bf16[512,512]{1,0:T(8,128)(2,1)S(1)} %copy-done.1, f32[512,512]{1,0:T(8,128)} %copy-done.6, f32[512,512]{1,0:T(8,128)S(1)} %fusion.21, f32[512,512]{1,0:T(8,128)} %copy-done.5), kind=kOutput, calls=%fused_computation.23 | convolution fusion | flops 271319040 | bytes 4194304 | tf_op jit(solution)/shard_map/dot_general | solution.py:104
  32.0 45.3 %reduce-scatter.8.cloned.1.call-done = bf16[512,32]{0,1:T(8,128)(2,1)} async-done(((bf16[512,512]{0,1:T(8,128)(2,1)}), bf16[512,32]{0,1:T(8,128)(2,1)}) %reduce-scatter.8.cloned.1.call-update) | async-done | bytes 32784 | tf_op jit(solution)/shard_map/reduce_scatter | solution.py:117
  78.8 1.9 collective-permute-start.3
  80.6 1.7 maximum_maximum_fusion
  82.4 1.8 fusion.28
  84.2 1.6 copy-done.4
  85.8 1.9 fusion.5
  87.7 51.6 %reduce-scatter.6.cloned.1.call-done = bf16[512,32]{0,1:T(8,128)(2,1)} async-done(((bf16[512,512]{0,1:T(8,128)(2,1)}), bf16[512,32]{0,1:T(8,128)(2,1)}) %reduce-scatter.6.cloned.1.call-update) | async-done | bytes 32784 | tf_op jit(solution)/shard_map/reduce_scatter | solution.py:114
  140.2 4.7 %fusion.6 = f32[512,512]{1,0:T(8,128)S(1)} fusion(bf16[2,1536,512]{2,1,0:T(8,128)(2,1)} %copy-done.3, f32[512,1536]{0,1:T(8,128)} %copy-done.4, f32[512]{0:T(512)S(1)} %fusion.5, f32[512]{0:T(512)S(1)} %get-tuple-element.12, s32[1536]{0:T(1024)S(1)} %iota_add_fusion, s32[512]{0:T(512)S(1)} %iota_add_fusion.1, s32[512]{0:T(512)S(1)} %convert_reduce_fusion.1, ...), kind=kOutput, calls=%fused_computation.13 | convolution fusion | flops 813957120 | bytes 5789184 | tf_op jit(solution)/shard_map/dot_general | solution.py:49
  144.9 55.8 %reduce-scatter.4.cloned.1.call-done = bf16[512,32]{0,1:T(8,128)(2,1)} async-done(((bf16[512,512]{0,1:T(8,128)(2,1)}), bf16[512,32]{0,1:T(8,128)(2,1)}) %reduce-scatter.4.cloned.1.call-update) | async-done | bytes 32784 | tf_op jit(solution)/shard_map/reduce_scatter | solution.py:111
  201.7 17.9 %all_gather.6 = bf16[512,512]{0,1:T(8,128)(2,1)S(1)} all-gather(bf16[512,32]{0,1:T(8,128)(2,1)S(1)} %subtract_convert_fusion.2), channel_id=1, replica_groups=mesh['seq'=16,'doc'=32] {'seq'}, dimensions={1}, use_global_device_ids=true | all-gather | bytes 557056 | tf_op jit(solution)/shard_map/all_gather | solution.py:134
  220.2 18.7 %all_gather.7 = bf16[512,512]{0,1:T(8,128)(2,1)} all-gather(bf16[512,32]{0,1:T(8,128)(2,1)S(1)} %subtract_convert_fusion.1), channel_id=1, replica_groups=mesh['seq'=16,'doc'=32] {'seq'}, dimensions={1}, use_global_device_ids=true | all-gather | bytes 557056 | tf_op jit(solution)/shard_map/all_gather | solution.py:135
  240.1 2.2 collective-permute-start.6
  245.6 2.6 collective-permute-start.9
  249.0 3.7 %collective-permute-start.11 = (bf16[512,32]{0,1:T(8,128)(2,1)S(1)}, bf16[512,32]{0,1:T(8,128)(2,1)S(1)}, u32[]{:S(2)}, u32[]{:S(2)}) collective-permute-start(bf16[512,32]{0,1:T(8,128)(2,1)S(1)} %collective-permute-done.9), channel_id=1, source_target_pairs={{0,480},{32,0},{64,32},{96,64},{128,96},{160,128},{192,160},{224,1... | collective-permute-start | bytes 98312 | tf_op jit(solution)/shard_map/ppermute | solution.py:22
  253.6 3.7 %collective-permute-start.13 = (bf16[512,32]{0,1:T(8,128)(2,1)S(1)}, bf16[512,32]{0,1:T(8,128)(2,1)S(1)}, u32[]{:S(2)}, u32[]{:S(2)}) collective-permute-start(bf16[512,32]{0,1:T(8,128)(2,1)S(1)} %collective-permute-done.11), channel_id=1, source_target_pairs={{0,480},{32,0},{64,32},{96,64},{128,96},{160,128},{192,160},{224,1... | collective-permute-start | bytes 98312 | tf_op jit(solution)/shard_map/ppermute | solution.py:22
  258.1 3.7 %collective-permute-start.15 = (bf16[512,32]{0,1:T(8,128)(2,1)S(1)}, bf16[512,32]{0,1:T(8,128)(2,1)S(1)}, u32[]{:S(2)}, u32[]{:S(2)}) collective-permute-start(bf16[512,32]{0,1:T(8,128)(2,1)S(1)} %collective-permute-done.13), channel_id=1, source_target_pairs={{0,480},{32,0},{64,32},{96,64},{128,96},{160,128},{192,160},{224,1... | collective-permute-start | bytes 98312 | tf_op jit(solution)/shard_map/ppermute | solution.py:22
  262.7 4.4 %collective-permute-done.16 = bf16[512,32]{0,1:T(8,128)(2,1)S(1)} collective-permute-done((bf16[512,32]{0,1:T(8,128)(2,1)S(1)}, bf16[512,32]{0,1:T(8,128)(2,1)S(1)}, u32[]{:S(2)}, u32[]{:S(2)}) %collective-permute-start.16) | collective-permute-done | bytes 32800 | tf_op jit(solution)/shard_map/ppermute | solution.py:19
  267.1 3.0 %multiply_reduce_fusion = (f32[512]{0:T(512)S(1)}, f32[512,512]{0,1:T(8,128)}) fusion(bf16[512,512]{0,1:T(8,128)(2,1)S(1)} %constant_dynamic-update-slice_fusion, bf16[512,512]{0,1:T(8,128)(2,1)} %all_gather.7, bf16[512,512]{1,0:T(8,128)(2,1)S(1)} %copy-done, f32[512,512]{1,0:T(8,128)S(1)} %convolution_bitcast_fusion.1), kind=kOutput, calls=%fused_computation.27 | convolution fusion | flops 538967552 | bytes 3672064 | tf_op jit(solution)/shard_map/dot_general | solution.py:141
  (107 shorter events, 20.4 us)
Async XLA Ops:
  7.2 75.2 %copy-start = (bf16[512,512]{1,0:T(8,128)(2,1)S(1)}, bf16[512,512]{1,0:T(8,128)(2,1)}, u32[]{:S(2)}) copy-start(bf16[512,512]{1,0:T(8,128)(2,1)} %param.12) | copy-start | bytes 1572868
  7.2 70.2 %reduce-scatter.8.cloned.1.call-start = ((), (), s32[]{:S(2)}) async-start(), calls=%async_computation.5 | async-start | bytes 557056 | tf_op jit(solution)/shard_map/reduce_scatter | solution.py:117
  13.5 125.7 %reduce-scatter.6.cloned.1.call-start = ((), (), s32[]{:S(2)}) async-start(), calls=%async_computation.4 | async-start | bytes 557056 | tf_op jit(solution)/shard_map/reduce_scatter | solution.py:114
  16.7 184.0 %reduce-scatter.4.cloned.1.call-start = ((), (), s32[]{:S(2)}) async-start(), calls=%async_computation.3 | async-start | bytes 557056 | tf_op jit(solution)/shard_map/reduce_scatter | solution.py:111
  17.8 62.8 %collective-permute-start.1 = (bf16[2,512,512]{2,1,0:T(8,128)(2,1)}, bf16[2,512,512]{2,1,0:T(8,128)(2,1)}, u32[]{:S(2)}, u32[]{:S(2)}) collective-permute-start(bf16[2,512,512]{2,1,0:T(8,128)(2,1)} %pad_maximum_fusion), channel_id=1, source_target_pairs={{0,32},{32,64},{64,96},{96,128},{128,160},{160,192},{192,224},{224... | collective-permute-start | bytes 3145736 | tf_op jit(solution)/shard_map/ppermute | solution.py:32
  22.5 58.1 %collective-permute-start = (bf16[2,512,512]{2,1,0:T(8,128)(2,1)}, bf16[2,512,512]{2,1,0:T(8,128)(2,1)}, u32[]{:S(2)}, u32[]{:S(2)}) collective-permute-start(bf16[2,512,512]{2,1,0:T(8,128)(2,1)} %pad_maximum_fusion), channel_id=1, source_target_pairs={{0,64},{32,96},{64,128},{96,160},{128,192},{160,224},{192,256},{22... | collective-permute-start | bytes 3145736 | tf_op jit(solution)/shard_map/ppermute | solution.py:32
  78.4 160.5 %collective-permute-start.2 = (bf16[512,32]{0,1:T(8,128)(2,1)S(1)}, bf16[512,32]{0,1:T(8,128)(2,1)S(1)}, u32[]{:S(2)}, u32[]{:S(2)}) collective-permute-start(bf16[512,32]{0,1:T(8,128)(2,1)S(1)} %get-tuple-element.9), channel_id=1, source_target_pairs={{0,32},{32,64},{64,96},{96,128},{128,160},{160,192},{192,224},{224... | collective-permute-start | bytes 98312 | tf_op jit(solution)/shard_map/ppermute | solution.py:19
  78.8 160.2 %collective-permute-start.3 = (bf16[512,32]{0,1:T(8,128)(2,1)S(1)}, bf16[512,32]{0,1:T(8,128)(2,1)S(1)}, u32[]{:S(2)}, u32[]{:S(2)}) collective-permute-start(bf16[512,32]{0,1:T(8,128)(2,1)S(1)} %get-tuple-element.9), channel_id=1, source_target_pairs={{0,480},{32,0},{64,32},{96,64},{128,96},{160,128},{192,160},{224,1... | collective-permute-start | bytes 98312 | tf_op jit(solution)/shard_map/ppermute | solution.py:22
  140.2 79.9 %copy-start.9 = (f32[512,32]{0,1:T(8,128)}, f32[512,32]{0,1:T(8,128)S(1)}, u32[]{:S(2)}) copy-start(f32[512,32]{0,1:T(8,128)S(1)} %get-tuple-element.7) | copy-start | bytes 196612
  140.2 60.5 %copy-start.13 = (f32[512,32]{0,1:T(8,128)S(1)}, f32[512,32]{0,1:T(8,128)}, u32[]{:S(2)}) copy-start(f32[512,32]{0,1:T(8,128)} %param.21) | copy-start | bytes 196612
  201.6 68.4 %copy-start.10 = (f32[512,32]{0,1:T(8,128)}, f32[512,32]{0,1:T(8,128)S(1)}, u32[]{:S(2)}) copy-start(f32[512,32]{0,1:T(8,128)S(1)} %get-tuple-element.5) | copy-start | bytes 196612
  238.9 1.2 collective-permute-start.4
  238.9 3.3 %collective-permute-start.5 = (bf16[512,32]{0,1:T(8,128)(2,1)S(1)}, bf16[512,32]{0,1:T(8,128)(2,1)S(1)}, u32[]{:S(2)}, u32[]{:S(2)}) collective-permute-start(bf16[512,32]{0,1:T(8,128)(2,1)S(1)} %collective-permute-done.3), channel_id=1, source_target_pairs={{0,480},{32,0},{64,32},{96,64},{128,96},{160,128},{192,160},{224,1... | collective-permute-start | bytes 98312 | tf_op jit(solution)/shard_map/ppermute | solution.py:22
  240.1 4.2 %collective-permute-start.6 = (bf16[512,32]{0,1:T(8,128)(2,1)S(1)}, bf16[512,32]{0,1:T(8,128)(2,1)S(1)}, u32[]{:S(2)}, u32[]{:S(2)}) collective-permute-start(bf16[512,32]{0,1:T(8,128)(2,1)S(1)} %collective-permute-done.4), channel_id=1, source_target_pairs={{0,32},{32,64},{64,96},{96,128},{128,160},{160,192},{192,224},{224... | collective-permute-start | bytes 98312 | tf_op jit(solution)/shard_map/ppermute | solution.py:19
  242.2 3.3 %collective-permute-start.7 = (bf16[512,32]{0,1:T(8,128)(2,1)S(1)}, bf16[512,32]{0,1:T(8,128)(2,1)S(1)}, u32[]{:S(2)}, u32[]{:S(2)}) collective-permute-start(bf16[512,32]{0,1:T(8,128)(2,1)S(1)} %collective-permute-done.5), channel_id=1, source_target_pairs={{0,480},{32,0},{64,32},{96,64},{128,96},{160,128},{192,160},{224,1... | collective-permute-start | bytes 98312 | tf_op jit(solution)/shard_map/ppermute | solution.py:22
  244.3 4.6 %collective-permute-start.8 = (bf16[512,32]{0,1:T(8,128)(2,1)S(1)}, bf16[512,32]{0,1:T(8,128)(2,1)S(1)}, u32[]{:S(2)}, u32[]{:S(2)}) collective-permute-start(bf16[512,32]{0,1:T(8,128)(2,1)S(1)} %collective-permute-done.6), channel_id=1, source_target_pairs={{0,32},{32,64},{64,96},{96,128},{128,160},{160,192},{192,224},{224... | collective-permute-start | bytes 98312 | tf_op jit(solution)/shard_map/ppermute | solution.py:19
  245.6 3.4 %collective-permute-start.9 = (bf16[512,32]{0,1:T(8,128)(2,1)S(1)}, bf16[512,32]{0,1:T(8,128)(2,1)S(1)}, u32[]{:S(2)}, u32[]{:S(2)}) collective-permute-start(bf16[512,32]{0,1:T(8,128)(2,1)S(1)} %collective-permute-done.7), channel_id=1, source_target_pairs={{0,480},{32,0},{64,32},{96,64},{128,96},{160,128},{192,160},{224,1... | collective-permute-start | bytes 98312 | tf_op jit(solution)/shard_map/ppermute | solution.py:22
  248.8 4.6 %collective-permute-start.10 = (bf16[512,32]{0,1:T(8,128)(2,1)S(1)}, bf16[512,32]{0,1:T(8,128)(2,1)S(1)}, u32[]{:S(2)}, u32[]{:S(2)}) collective-permute-start(bf16[512,32]{0,1:T(8,128)(2,1)S(1)} %collective-permute-done.8), channel_id=1, source_target_pairs={{0,32},{32,64},{64,96},{96,128},{128,160},{160,192},{192,224},{224... | collective-permute-start | bytes 98312 | tf_op jit(solution)/shard_map/ppermute | solution.py:19
  249.0 4.6 %collective-permute-start.11 = (bf16[512,32]{0,1:T(8,128)(2,1)S(1)}, bf16[512,32]{0,1:T(8,128)(2,1)S(1)}, u32[]{:S(2)}, u32[]{:S(2)}) collective-permute-start(bf16[512,32]{0,1:T(8,128)(2,1)S(1)} %collective-permute-done.9), channel_id=1, source_target_pairs={{0,480},{32,0},{64,32},{96,64},{128,96},{160,128},{192,160},{224,1... | collective-permute-start | bytes 98312 | tf_op jit(solution)/shard_map/ppermute | solution.py:22
  253.4 4.6 %collective-permute-start.12 = (bf16[512,32]{0,1:T(8,128)(2,1)S(1)}, bf16[512,32]{0,1:T(8,128)(2,1)S(1)}, u32[]{:S(2)}, u32[]{:S(2)}) collective-permute-start(bf16[512,32]{0,1:T(8,128)(2,1)S(1)} %collective-permute-done.10), channel_id=1, source_target_pairs={{0,32},{32,64},{64,96},{96,128},{128,160},{160,192},{192,224},{224... | collective-permute-start | bytes 98312 | tf_op jit(solution)/shard_map/ppermute | solution.py:19
  253.6 4.6 %collective-permute-start.13 = (bf16[512,32]{0,1:T(8,128)(2,1)S(1)}, bf16[512,32]{0,1:T(8,128)(2,1)S(1)}, u32[]{:S(2)}, u32[]{:S(2)}) collective-permute-start(bf16[512,32]{0,1:T(8,128)(2,1)S(1)} %collective-permute-done.11), channel_id=1, source_target_pairs={{0,480},{32,0},{64,32},{96,64},{128,96},{160,128},{192,160},{224,1... | collective-permute-start | bytes 98312 | tf_op jit(solution)/shard_map/ppermute | solution.py:22
  257.9 4.6 %collective-permute-start.14 = (bf16[512,32]{0,1:T(8,128)(2,1)S(1)}, bf16[512,32]{0,1:T(8,128)(2,1)S(1)}, u32[]{:S(2)}, u32[]{:S(2)}) collective-permute-start(bf16[512,32]{0,1:T(8,128)(2,1)S(1)} %collective-permute-done.12), channel_id=1, source_target_pairs={{0,32},{32,64},{64,96},{96,128},{128,160},{160,192},{192,224},{224... | collective-permute-start | bytes 98312 | tf_op jit(solution)/shard_map/ppermute | solution.py:19
  258.1 4.6 %collective-permute-start.15 = (bf16[512,32]{0,1:T(8,128)(2,1)S(1)}, bf16[512,32]{0,1:T(8,128)(2,1)S(1)}, u32[]{:S(2)}, u32[]{:S(2)}) collective-permute-start(bf16[512,32]{0,1:T(8,128)(2,1)S(1)} %collective-permute-done.13), channel_id=1, source_target_pairs={{0,480},{32,0},{64,32},{96,64},{128,96},{160,128},{192,160},{224,1... | collective-permute-start | bytes 98312 | tf_op jit(solution)/shard_map/ppermute | solution.py:22
  262.5 4.6 %collective-permute-start.16 = (bf16[512,32]{0,1:T(8,128)(2,1)S(1)}, bf16[512,32]{0,1:T(8,128)(2,1)S(1)}, u32[]{:S(2)}, u32[]{:S(2)}) collective-permute-start(bf16[512,32]{0,1:T(8,128)(2,1)S(1)} %collective-permute-done.14), channel_id=1, source_target_pairs={{0,32},{32,64},{64,96},{96,128},{128,160},{160,192},{192,224},{224... | collective-permute-start | bytes 98312 | tf_op jit(solution)/shard_map/ppermute | solution.py:19
  (13 other events, 156.7 us)
Sparse Core Ops, SparseCore 0:
  13.7 63.6 reduce-scatter.7
  80.1 59.1 reduce-scatter.5
  142.1 58.5 reduce-scatter.3
